TPU v7x, 256 devices: a whole 4x4x8 slice. The times are simulated.
256 devices in a mesh: tile: 8 (over y, core), freq: 32 (over x, z).
Axes of the slice: x: 4, y: 4, z: 8, core: 2. Of those that a mesh axis runs over, the one named last changes fastest.
Arguments:
- sensitivity: float32 [8, 32, 2, 1024, 512], P('tile', 'freq'), may hold values from -0.25 to 0.25
- models: float32 [2048, 256], P(('tile', 'freq')), may hold values from -6 to 6
- observed: float32 [8, 40, 1024], P('tile', None, 'freq'), may hold values from -6 to 6
- waveform: float32 [128], replicated, may hold values from -0.5 to 0.5
- cell_index: int32 [8, 512], P('tile'), may hold values from 0 to 2047, as said below
- gate_index: int32 [40], replicated, may hold values from 10 to 127, as said below
Outputs:
- updated: float32 [2048, 256], P(('tile', 'freq'))
- misfit: float32 [256], replicated
Inputs may be any that keep to these rules, and one draw needn't show every extreme that they name: `cell_index`: each tile's indices are distinct. Tile t holds, in some order, the 256 global cells from t * 256 on and the 256 cells of one other tile's block (from u * 256 on, u != t). Every global cell belongs to one or more tiles. `gate_index`: strictly increasing; the last gate is sample 128 - 1.
All inputs are finite; a program needn't handle non-finite values.
Results may differ from a plain program's by a relative error of at most 0.00017.
Values sent between devices are 32-bit elements; how exact they have to be, the bound alone decides.
A program may use at most 64 MiB of HBM per device.

v0:
```python
import math

import jax
import jax.numpy as jnp
from jax import lax
from jax.sharding import PartitionSpec as P

HIGH = lax.Precision.HIGHEST
PHASE_RATE = 0.37
STEP_LENGTH = 0.5
EPSILON = 1e-06


def gate_tables(freqs, waveform, gate_index):
    samples = waveform.shape[0]
    freq_col = jnp.arange(freqs, dtype=jnp.float32)[:, None] + 0.5
    time_row = jnp.arange(samples, dtype=jnp.float32)[None, :] + 0.5
    phases = PHASE_RATE * freq_col * time_row
    kernel = jnp.stack([jnp.cos(phases), jnp.sin(phases)], axis=1) / math.sqrt(freqs)
    time_lag = jnp.arange(samples)[:, None] - jnp.arange(samples)[None, :]
    toeplitz = jnp.where(time_lag >= 0, jnp.take(waveform, jnp.clip(time_lag, 0, samples - 1)), 0.0)
    picker = (gate_index[:, None] == jnp.arange(samples)[None, :]).astype(jnp.float32)
    return (kernel, toeplitz, picker)


def body(sensitivity, models, observed, waveform, cell_index, gate_index):
    freqs = sensitivity.shape[1] * lax.axis_size("freq")
    soundings = sensitivity.shape[3]
    members = models.shape[1]
    gates = gate_index.shape[0]
    devices = lax.axis_size(("tile", "freq"))
    owned_count = models.shape[0]
    ncells = owned_count * devices
    total = lax.axis_size("tile") * soundings * gates
    kernel, toeplitz, picker = gate_tables(freqs, waveform, gate_index)
    block = sensitivity[0]
    all_models = lax.all_gather(models, ("tile", "freq"), axis=0, tiled=True)
    tile_cells = cell_index[0]
    tile_models = jnp.take(all_models, tile_cells, axis=0)
    predicted = jnp.einsum("fpsc,cm->fpsm", block, tile_models, precision=HIGH)
    spectra = lax.all_to_all(predicted, "freq", split_axis=2, concat_axis=0, tiled=True)
    series = jnp.einsum("fpk,fpsm->ksm", kernel, spectra, precision=HIGH)
    series = jnp.einsum("kj,jsm->ksm", toeplitz, series, precision=HIGH)
    response = jnp.einsum("gk,ksm->gsm", picker, series, precision=HIGH)
    misfit_rows = response - observed[0][:, :, None]
    partial_misfit = jnp.sum(misfit_rows * misfit_rows, axis=(0, 1))
    misfit_total = lax.psum(partial_misfit, ("tile", "freq"))
    upward = jnp.einsum("gk,gsm->ksm", picker, misfit_rows, precision=HIGH)
    upward = jnp.einsum("kj,ksm->jsm", toeplitz, upward, precision=HIGH)
    back = jnp.einsum("fpk,ksm->fpsm", kernel, upward, precision=HIGH)
    back_spectra = lax.all_to_all(back, "freq", split_axis=0, concat_axis=2, tiled=True)
    cell_terms = jnp.einsum("fpsc,fpsm->cm", block, back_spectra, precision=HIGH)
    scattered = jnp.zeros((ncells, members), jnp.float32).at[tile_cells].add(cell_terms)
    summed = lax.psum(scattered, ("tile", "freq"))
    gradient = lax.dynamic_slice_in_dim(
        summed, lax.axis_index(("tile", "freq")) * owned_count, owned_count, 0
    )
    partial_square = jnp.sum(gradient * gradient, axis=0)
    square_total = lax.psum(partial_square, ("tile", "freq"))
    misfit = misfit_total / (2.0 * total)
    scale = jnp.sqrt(square_total / ncells + EPSILON)
    updated = models - STEP_LENGTH * (misfit / scale)[None, :] * gradient
    return (updated, misfit)


def solution(mesh):
    in_specs = (
        P("tile", "freq", None, None, None),
        P(("tile", "freq"), None),
        P("tile", None, "freq"),
        P(),
        P("tile", None),
        P(),
    )
    out_specs = (P(("tile", "freq"), None), P())
    return jax.shard_map(body, mesh=mesh, in_specs=in_specs, out_specs=out_specs, check_vma=False)
```

profile of v0, /device:TPU:1, one launch (start us, length us, event | category | flops | bytes accessed | tf_op | source)
XLA Modules:
  0.0 677.4 jit_solution(5995075499652823662)
XLA Ops:
  7.2 0.7 all-gather.2.cloned.1.call-update
  7.9 0.7 compare_select_fusion.2
  8.6 0.7 compare_and_fusion
  9.3 110.7 %all-gather.2.cloned.1.call-done = f32[2048,256]{1,0:T(8,128)} async-done(((f32[8,256]{1,0:T(8,128)}), f32[2048,256]{1,0:T(8,128)}) %all-gather.2.cloned.1.call-update) | async-done | bytes 2097168 | tf_op jit(solution)/shard_map/all_gather | solution.py:37
  120.0 3.2 gather_fusion.1
  123.2 9.0 %fusion.11 = f32[1,2,1024,256]{2,3,1,0:T(8,128)S(1)} fusion(f32[1,1,2,1024,512]{4,3,2,1,0:T(8,128)} %param.6, f32[512,256]{1,0:T(8,128)S(1)} %gather_fusion.1, pred[512]{0:T(512)(128)(4,1)S(1)} %compare_and_fusion), kind=kOutput, calls=%fused_computation.14 | convolution fusion | flops 3221356544 | bytes 6816256 | tf_op jit(solution)/shard_map/fpsc,cm->fpsm/dot_general | solution.py:40
  132.2 2.4 copy.25
  134.6 7.4 %all-to-all-start = ((f32[1,2,1024,256]{3,1,0,2:T(2,128)}), f32[1,2,1024,256]{3,1,0,2:T(2,128)S(1)}, u32[]{:S(2)}, u32[]{:S(2)}) async-start(f32[1,2,1024,256]{3,1,0,2:T(2,128)} %copy.25), calls=%async_computation | async-start | bytes 4194304 | tf_op jit(solution)/shard_map/all_to_all | solution.py:41
  142.1 97.4 %gather_fusion = f32[16384]{0:T(1024)S(1)} fusion(f32[128]{0:T(128)S(1)} %copy-done, s32[16384]{0:T(1024)S(1)} %fusion.24), kind=kCustom, calls=%fused_computation | custom fusion | bytes 196608 | tf_op jit(solution)/shard_map/jit(_take)/gather | solution.py:21
  239.7 4.7 fusion.8
  244.3 4.0 fusion.2
  248.4 1.9 multiply_reduce_fusion
  250.3 1.9 fusion.38
  252.2 4.3 fusion.25
  256.5 2.3 fusion
  258.8 1.2 copy.29
  260.1 56.3 %all_to_all.33 = f32[32,2,32,256]{3,2,1,0:T(8,128)S(1)} all-to-all(f32[32,2,32,256]{3,2,1,0:T(8,128)S(1)} %copy.29), channel_id=1, replica_groups=mesh['tile'=8,'freq'=32] {'freq'}, dimensions={0} | all-to-all | bytes 4194304 | tf_op jit(solution)/shard_map/all_to_all | solution.py:51
  316.6 1.9 copy-done.1
  318.5 3.8 fusion.14
  322.6 4.7 scatter_custom_fusion
  327.3 263.0 %all-reduce.3.cloned.1.call-done = f32[2048,256]{1,0:T(8,128)} async-done(((f32[2048,256]{1,0:T(8,128)}), f32[2048,256]{1,0:T(8,128)}) %all-reduce.3.cloned.1.call-update) | async-done | bytes 2097168 | tf_op jit(solution)/shard_map/psum | solution.py:54
  590.3 0.7 multiply_reduce_fusion.1
  591.0 77.7 %all-reduce = (f32[256]{0:T(256)S(1)}, f32[256]{0:T(256)S(1)}) all-reduce(f32[256]{0:T(256)S(1)} %get-tuple-element.8, f32[256]{0:T(256)S(1)} %multiply_reduce_fusion.1), channel_id=1, replica_groups=mesh['tile'=8,'freq'=32] {'tile','freq'}, use_global_device_ids=true, to_apply=%region_1.2 | all-reduce | flops 512 | bytes 4096 | tf_op jit(solution)/shard_map/psum | solution.py:47
  669.3 1.3 multiply_subtract_fusion
  (21 shorter events, 1.3 us)
Async XLA Ops:
  7.2 134.9 %copy-start = (f32[128]{0:T(128)S(1)}, f32[128]{0:T(128)}, u32[]{:S(2)}) copy-start(f32[128]{0:T(128)} %param.9) | copy-start | bytes 1540
  7.2 112.9 %all-gather.2.cloned.1.call-start = ((), (), s32[]{:S(2)}) async-start(), calls=%async_computation.2 | async-start | bytes 2105344 | tf_op jit(solution)/shard_map/all_gather | solution.py:37
  134.6 105.1 %all-to-all-start = ((f32[1,2,1024,256]{3,1,0,2:T(2,128)}), f32[1,2,1024,256]{3,1,0,2:T(2,128)S(1)}, u32[]{:S(2)}, u32[]{:S(2)}) async-start(f32[1,2,1024,256]{3,1,0,2:T(2,128)} %copy.25), calls=%async_computation | async-start | bytes 4194304 | tf_op jit(solution)/shard_map/all_to_all | solution.py:41
  142.0 448.3 %all-reduce.3.cloned.1.call-start = ((), (), s32[]{:S(2)}) async-start(), calls=%async_computation.3 | async-start | bytes 4194304 | tf_op jit(solution)/shard_map/psum | solution.py:54
  244.3 4.1 copy-start.3
  244.3 4.1 copy-start.4
  316.3 2.2 copy-start.1
  322.6 346.7 %copy-start.2 = (f32[8,256]{1,0:T(8,128)S(1)}, f32[8,256]{1,0:T(8,128)}, u32[]{:S(2)}) copy-start(f32[8,256]{1,0:T(8,128)} %param.7) | copy-start | bytes 24580
Sparse Core Ops, SparseCore 0:
  11.7 108.2 all-gather.1
  327.4 262.8 all-reduce.2
where the time goes:
time: 678 us; the launch traced here: 677 us
  waiting for transfers between devices  374 us (55%)
  blocking collectives  134 us (20%)
  local copies, waits for them, and re-layouts  107 us (16%)
  matrix products  31.9 us (5%)
  between operations  14.2 us (2%)
  other arithmetic  8.85 us (1%)
  starting transfers between devices  7.46 us (1%)
    psum x1, waiting for transfers between devices, body(): summed = lax.psum(scattered, ('tile', 'freq'))  263 us
    all_gather x1, waiting for transfers between devices, body(): all_models = lax.all_gather(models, ('tile', 'freq'), axis=0, tiled=True)  111 us
    gather x1, local copies, waits for them, and re-layouts, gate_tables(): jnp.take(waveform, jnp.clip(time_lag, 0, samples - 1))  97.4 us
    psum x1, blocking collectives, body(): misfit_total = lax.psum(partial_misfit, ('tile', 'freq'))  77.7 us
    all_to_all x1, blocking collectives, body(): lax.all_to_all(back, 'freq', split_axis=0, concat_axis=2, tiled=True)  56.3 us
  transfers between devices with their start and end apart: 3, of which 2 were waited for; matrix products, arithmetic and copies ran while one was open for 15% of the time, Pallas kernels for 0%

commit v1 on v0

v1 whole, which is shorter than its diff:
```python
import functools
import math

import jax
import jax.numpy as jnp
import numpy as np
from jax import lax
from jax.experimental import pallas as pl
from jax.experimental.pallas import tpu as pltpu
from jax.sharding import PartitionSpec as P

HIGH = lax.Precision.HIGHEST
PHASE_RATE = 0.37
STEP_LENGTH = 0.5
EPSILON = 1e-06
MESH = pl.DeviceIdType.MESH
NX, NZ, NT = 4, 8, 8
NF = NX * NZ
ROWS = 8
F32, BF16 = jnp.float32, jnp.bfloat16


def kernel_table(freqs, samples):
    freq_col = np.arange(freqs, dtype=np.float32)[:, None] + np.float32(0.5)
    time_row = np.arange(samples, dtype=np.float32)[None, :] + np.float32(0.5)
    phases = ((np.float32(PHASE_RATE) * freq_col) * time_row).astype(np.float64)
    table = np.stack([np.cos(phases), np.sin(phases)], axis=1) / math.sqrt(freqs)
    return table.reshape(2 * freqs, samples).astype(np.float32)


def nn(a, b, precision=None):
    return lax.dot_general(a, b, (((1,), (0,)), ((), ())), precision=precision, preferred_element_type=F32)


def nt(a, b, precision=None):
    return lax.dot_general(a, b, (((1,), (1,)), ((), ())), precision=precision, preferred_element_type=F32)


def split(a):
    high = a.astype(BF16)
    return high, (a - high.astype(F32)).astype(BF16)


def three(dot, a, b):
    return dot(a[0], b[0]) + dot(a[0], b[1]) + dot(a[1], b[0])


def iota(shape, dim):
    return lax.broadcasted_iota(jnp.int32, shape, dim)


def await_bytes(ref, sem):
    pltpu.make_async_copy(ref, ref, sem).wait()


def kernel(
    wave_ref, gate_ref, sens_ref, models_ref, obs_ref, cell_ref, table_ref,
    out_ref, misfit_ref,
    buf, tiles, gathered, wide, expanded, onehot, model_t, cells_t, grads, xrecv, zsend, zrecv, tsend, trecv,
    square_row, square_rows, misfit_row, misfit_rows, final_row, final_rows,
    bulk_send, bulk_recv, send, recv, pair_send, pair_recv,
):
    tile = lax.axis_index("tile")
    f = lax.axis_index("freq")
    x, z = f // NZ, lax.rem(f, NZ)
    chunks = buf.shape[0]
    soundings = chunks * ROWS
    gates = obs_ref.shape[1]
    total = NT * NF * soundings * gates
    ncells = NT * NF * ROWS

    def plane(i):
        return {"freq": lax.rem(x + i // NZ, NX) * NZ + lax.rem(z + i % NZ, NZ)}

    def other_tile(i):
        return {"tile": lax.rem(tile + i, NT)}

    def put(src, dst, send_sem, recv_sem, device):
        pltpu.make_async_remote_copy(
            src_ref=src, dst_ref=dst, send_sem=send_sem, recv_sem=recv_sem, device_id=device, device_id_type=MESH
        ).start()

    barrier = pltpu.get_barrier_semaphore()
    for i in range(1, NF):
        pl.semaphore_signal(barrier, inc=1, device_id=plane(i), device_id_type=MESH)
    for i in range(1, NT):
        pl.semaphore_signal(barrier, inc=1, device_id=other_tile(i), device_id_type=MESH)
    pl.semaphore_wait(barrier, NF + NT - 2)

    for i in range(1, NT):
        put(models_ref, tiles.at[tile], send.at[0], recv.at[0], other_tile(i))

    def send_chunk(c):
        for i in range(1, NF):
            p = plane(i)
            start = pl.multiple_of(p["freq"] * soundings + c * ROWS, ROWS)
            put(sens_ref.at[0, 0, :, pl.ds(start, ROWS), :], buf.at[c, f], bulk_send.at[c], bulk_recv.at[c], p)
        start = pl.multiple_of(f * soundings + c * ROWS, ROWS)
        pltpu.make_async_copy(sens_ref.at[0, 0, :, pl.ds(start, ROWS), :], buf.at[c, f], bulk_recv.at[c]).start()

    send_chunk(0)

    cells = cell_ref[...]
    block = lax.shift_right_logical(cells, 8)
    partner = jnp.max(jnp.where(block != tile, block, -1), axis=1, keepdims=True)
    local = jnp.where(block == tile, cells & 255, 256 + (cells & 255))
    ncell = cells.shape[1]
    onehot[...] = jnp.where(iota((ncell, ncell), 0) == local, 1.0, 0.0).astype(BF16)

    tiles[tile] = models_ref[...]
    await_bytes(tiles.at[pl.ds(0, NT - 1)], recv.at[0])
    borrowed = jnp.zeros_like(models_ref)
    for t in range(NT):
        borrowed = jnp.where(partner == t, tiles[t], borrowed)
    gathered[x, z, 0] = models_ref[...]
    gathered[x, z, 1] = borrowed
    for i in range(1, NZ):
        put(gathered.at[x, z], gathered.at[x, z], send.at[1], recv.at[1], plane(i))
    send_chunk(1)

    samples = table_ref.shape[1]
    rows = iota((gates, samples), 0)
    lag = lax.fori_loop(0, gates, lambda g, a: jnp.where(rows == g, gate_ref[g], a), jnp.zeros((gates, samples), jnp.int32))
    lag = lag - iota((gates, samples), 1)
    toeplitz = lax.fori_loop(
        0, samples, lambda k, a: jnp.where(lag == k, wave_ref[k], a), jnp.zeros((gates, samples), F32)
    )
    narrow = nt(toeplitz, table_ref[...], HIGH)
    spread = jnp.where(lax.shift_right_logical(iota((gates * ROWS, gates), 0), 3) == iota((gates * ROWS, gates), 1), 1.0, 0.0)
    fps = narrow.shape[1]
    pick = jnp.where(iota((fps, fps * ROWS), 0) == lax.shift_right_logical(iota((fps, fps * ROWS), 1), 3), 1.0, 0.0)
    big = nn(nn(spread, narrow, HIGH), pick, HIGH)
    same = (iota(big.shape, 0) & 7) == (iota(big.shape, 1) & 7)
    big_high, big_low = split(jnp.where(same, big, 0.0))
    wide[0] = big_high
    wide[1] = big_low
    expanded[...] = nn(spread, obs_ref[0], HIGH)

    await_bytes(gathered.at[0, pl.ds(0, NZ - 1)], recv.at[1])
    for i in range(1, NX):
        put(gathered.at[x], gathered.at[x], send.at[2], recv.at[2], plane(i * NZ))
    send_chunk(2)
    send_chunk(3)

    await_bytes(gathered.at[pl.ds(0, NX - 1)], recv.at[2])
    for b in range(2):
        part = gathered[:, :, b].reshape(NF * ROWS, -1)
        part_high, part_low = split(part.T)
        hot = onehot[pl.ds(b * NF * ROWS, NF * ROWS), :]
        if b == 0:
            model_high, model_low = nn(part_high, hot), nn(part_low, hot)
        else:
            model_high, model_low = model_high + nn(part_high, hot), model_low + nn(part_low, hot)
    model_t[0] = model_high.astype(BF16)
    model_t[1] = model_low.astype(BF16)

    cells_t[...] = jnp.zeros_like(cells_t)
    misfit_row[...] = jnp.zeros_like(misfit_row)

    def chunk(c, carry):
        await_bytes(buf.at[c], bulk_recv.at[c])
        block_s = split(buf[c].reshape(fps * ROWS, ncell))
        operator = split(three(nn, (wide[0], wide[1]), block_s))
        seen = expanded[...]
        seen = jnp.where(iota(seen.shape, 1) == c * ROWS + (iota(seen.shape, 0) & 7), seen, 0.0)
        seen_row = nt(jnp.ones((8, seen.shape[1]), F32), seen, HIGH)[0:1]
        rows_t = three(nt, (model_t[0], model_t[1]), operator) - seen_row
        misfit_row[...] += nt(jnp.ones((8, rows_t.shape[1]), F32), rows_t * rows_t, HIGH)[0:1]
        cells_t[...] += three(nn, split(rows_t), operator)
        return carry

    lax.fori_loop(0, chunks, chunk, 0)

    grad_high, grad_low = split(cells_t[...])
    half = NF * ROWS
    for b in (1, 0):
        hot = onehot[pl.ds(b * half, half), :]
        part = nt(hot, grad_high) + nt(hot, grad_low)
        grads[b] = part.reshape(NX, NZ, ROWS, -1)
        for i in range(1, NX):
            p = lax.rem(x + i, NX)
            put(grads.at[b, p], xrecv.at[b, x], pair_send.at[0, b], pair_recv.at[0, b], plane(i * NZ))
    for i in range(1, NF):
        put(misfit_row, misfit_rows.at[f], send.at[3], recv.at[3], plane(i))
    for b in (1, 0):
        xrecv[b, x] = grads[b, x]
        await_bytes(xrecv.at[b, pl.ds(0, NX - 1)], pair_recv.at[0, b])
        zsend[b] = (xrecv[b, 0] + xrecv[b, 1]) + (xrecv[b, 2] + xrecv[b, 3])
        for i in range(1, NZ):
            p = lax.rem(z + i, NZ)
            put(zsend.at[b, p], zrecv.at[b, z], pair_send.at[1, b], pair_recv.at[1, b], plane(i))
    sums = []
    for b in (1, 0):
        zrecv[b, z] = zsend[b, z]
        await_bytes(zrecv.at[b, pl.ds(0, NZ - 1)], pair_recv.at[1, b])
        sums.append(jnp.sum(zrecv[b], axis=0))
        if b == 1:
            for t in range(NT):
                tsend[t] = jnp.where(partner == t, sums[0], 0.0)
            for i in range(1, NT):
                put(tsend.at[lax.rem(tile + i, NT)], trecv.at[tile], send.at[4], recv.at[4], other_tile(i))
    trecv[tile] = jnp.zeros_like(sums[0])
    await_bytes(trecv.at[pl.ds(0, NT - 1)], recv.at[4])
    gradient = sums[1] + jnp.sum(trecv[...], axis=0)

    square_row[...] = jnp.sum(gradient * gradient, axis=0, keepdims=True)
    for i in range(1, NF):
        put(square_row, square_rows.at[f], send.at[5], recv.at[5], plane(i))
    square_rows[f] = square_row[...]
    misfit_rows[f] = misfit_row[...]
    await_bytes(misfit_rows.at[pl.ds(0, NF - 1)], recv.at[3])
    members = misfit_row.shape[1]
    final_row[:, pl.ds(members, members)] = jnp.sum(misfit_rows[...], axis=0)
    await_bytes(square_rows.at[pl.ds(0, NF - 1)], recv.at[5])
    final_row[:, pl.ds(0, members)] = jnp.sum(square_rows[...], axis=0)
    for i in range(1, NT):
        put(final_row, final_rows.at[tile], send.at[6], recv.at[6], other_tile(i))
    final_rows[tile] = final_row[...]
    await_bytes(final_rows.at[pl.ds(0, NT - 1)], recv.at[6])
    final = jnp.sum(final_rows[...], axis=0)
    misfit = final[:, members:] / (2.0 * total)
    scale = jnp.sqrt(final[:, :members] / ncells + EPSILON)
    out_ref[...] = models_ref[...] - STEP_LENGTH * (misfit / scale) * gradient
    misfit_ref[...] = misfit

    for c in range(chunks):
        await_bytes(buf.at[c, pl.ds(0, NF - 1)], bulk_send.at[c])
    await_bytes(tiles.at[pl.ds(0, NT - 1)], send.at[0])
    await_bytes(gathered.at[0, pl.ds(0, NZ - 1)], send.at[1])
    await_bytes(gathered.at[pl.ds(0, NX - 1)], send.at[2])
    await_bytes(misfit_rows.at[pl.ds(0, NF - 1)], send.at[3])
    await_bytes(trecv.at[pl.ds(0, NT - 1)], send.at[4])
    await_bytes(square_rows.at[pl.ds(0, NF - 1)], send.at[5])
    await_bytes(final_rows.at[pl.ds(0, NT - 1)], send.at[6])
    for b in range(2):
        await_bytes(xrecv.at[b, pl.ds(0, NX - 1)], pair_send.at[0, b])
        await_bytes(zrecv.at[b, pl.ds(0, NZ - 1)], pair_send.at[1, b])


def body(sensitivity, models, observed, waveform, cell_index, gate_index):
    owned, members = models.shape
    gates = gate_index.shape[0]
    ncell = cell_index.shape[1]
    chunks = sensitivity.shape[3] // NF // ROWS
    table = jnp.asarray(kernel_table(NF, waveform.shape[0]))
    vmem, smem = pl.BlockSpec(memory_space=pltpu.VMEM), pl.BlockSpec(memory_space=pltpu.SMEM)
    dma = pltpu.SemaphoreType.DMA
    updated, misfit = pl.pallas_call(
        kernel,
        out_shape=(jax.ShapeDtypeStruct((owned, members), F32), jax.ShapeDtypeStruct((1, members), F32)),
        in_specs=[smem, smem, pl.BlockSpec(memory_space=pl.ANY), vmem, vmem, vmem, vmem],
        out_specs=(vmem, vmem),
        scratch_shapes=[
            pltpu.VMEM((chunks, NF, 2, ROWS, ncell), F32),
            pltpu.VMEM((NT, ROWS, members), F32),
            pltpu.VMEM((NX, NZ, 2, ROWS, members), F32),
            pltpu.VMEM((2, gates * ROWS, 2 * NF * ROWS), BF16),
            pltpu.VMEM((gates * ROWS, chunks * ROWS), F32),
            pltpu.VMEM((ncell, ncell), BF16),
            pltpu.VMEM((2, members, ncell), BF16),
            pltpu.VMEM((members, ncell), F32),
            pltpu.VMEM((2, NX, NZ, ROWS, members), F32),
            pltpu.VMEM((2, NX, NZ, ROWS, members), F32),
            pltpu.VMEM((2, NZ, ROWS, members), F32),
            pltpu.VMEM((2, NZ, ROWS, members), F32),
            pltpu.VMEM((NT, ROWS, members), F32),
            pltpu.VMEM((NT, ROWS, members), F32),
            pltpu.VMEM((1, members), F32),
            pltpu.VMEM((NF, 1, members), F32),
            pltpu.VMEM((1, members), F32),
            pltpu.VMEM((NF, 1, members), F32),
            pltpu.VMEM((1, 2 * members), F32),
            pltpu.VMEM((NT, 1, 2 * members), F32),
            dma((chunks,)), dma((chunks,)), dma((7,)), dma((7,)), dma((2, 2)), dma((2, 2)),
        ],
        compiler_params=pltpu.CompilerParams(collective_id=0, has_side_effects=True, vmem_limit_bytes=60 << 20),
    )(waveform, gate_index, sensitivity, models, observed, cell_index, table)
    return updated, misfit[0]


def solution(mesh):
    in_specs = (
        P("tile", "freq", None, None, None),
        P(("tile", "freq"), None),
        P("tile", None, "freq"),
        P(),
        P("tile", None),
        P(),
    )
    out_specs = (P(("tile", "freq"), None), P())
    return jax.shard_map(body, mesh=mesh, in_specs=in_specs, out_specs=out_specs, check_vma=False)
```

time: 678 us -> 140 us (0.21)
  waiting for transfers between devices: 374 us -> 0 us
  Pallas kernels: 0 us -> 135 us
  blocking collectives: 134 us -> 0 us
  local copies, waits for them, and re-layouts: 107 us -> 3.89 us
  matrix products: 31.9 us -> 0 us
  between operations: 14.2 us -> 0.64 us
  other arithmetic: 8.85 us -> 0 us
  starting transfers between devices: 7.46 us -> 0 us
    psum x1 -> x0, waiting for transfers between devices: 263 us -> none  [body(): summed = lax.psum(scattered, ('tile', 'freq'))]
    pallas_call x0 -> x1, Pallas kernels: none -> 135 us  [body(): pl.pallas_call(kernel, out_shape=(jax.ShapeDtypeStruct((owned, members),...]
    all_gather x1 -> x0, waiting for transfers between devices: 111 us -> none  [body(): all_models = lax.all_gather(models, ('tile', 'freq'), axis=0, tiled=True)]
    gather x2 -> x0, local copies, waits for them, and re-layouts: 101 us -> none  [the longest x1 97.4 us: gate_tables(): jnp.take(waveform, jnp.clip(time_lag, 0, samples - 1))]
    psum x1 -> x0, blocking collectives: 77.7 us -> none  [body(): misfit_total = lax.psum(partial_misfit, ('tile', 'freq'))]
    all_to_all x1 -> x0, blocking collectives: 56.3 us -> none  [body(): lax.all_to_all(back, 'freq', split_axis=0, concat_axis=2, tiled=True)]
    dot_general x8 -> x0, matrix products: 31.9 us -> none  [the longest x1 9.02 us: body(): predicted = jnp.einsum('fpsc,cm->fpsm', block, tile_models, precision=HIGH)]
    all_to_all x1 -> x0, starting transfers between devices: 7.38 us -> none  [body(): lax.all_to_all(predicted, 'freq', split_axis=2, concat_axis=0, tiled=True)]
  transfers between devices with their start and end apart: 3 -> 0, of which waited for: 2 -> 0; matrix products, arithmetic and copies ran while one was open for 15% -> 0% of each run, Pallas kernels for 0% -> 0%
where the time goes in v1:
time: 140 us
  Pallas kernels  135 us (96%)
  local copies, waits for them, and re-layouts  3.89 us (3%)
    pallas_call x1, Pallas kernels, body(): pl.pallas_call(kernel, out_shape=(jax.ShapeDtypeStruct((owned, members),...  135 us
    unnamed x3, local copies, waits for them, and re-layouts  3.89 us

profile of v1, /device:TPU:1, one launch (start us, length us, event | category | flops | bytes accessed | tf_op | source)
XLA Modules:
  0.0 139.9 jit_solution(18002023232351748768)
XLA Ops:
  0.6 1.4 copy.9.obs_ref
  2.0 135.4 %shard_map.86 = (f32[8,256]{1,0:T(8,128)}, f32[1,256]{1,0:T(1,128)}) custom-call(f32[128]{0:T(128)} %wave_ref.1, s32[40]{0:T(128)} %gate_ref.1, f32[1,1,2,1024,512]{4,3,2,1,0:T(8,128)} %sens_ref.1, f32[8,256]{1,0:T(8,128)} %models_ref.1, f32[1,40,32]{2,1,0:T(8,128)} %copy.9.obs_ref, s32[1,512]{1,0:T(1,128)} %cell_ref.1, f32[64,128]{1,0:T(8,128)} %constant.2.clone.table_ref), custom_call_target="tpu_custom_call" | custom-call | tf_op jit(solution)/shard_map/pallas_call | solution.py:248
  137.4 1.3 copy.12
  138.7 1.2 copy.13

commit v2 on v1

--- a/solution.py
+++ b/solution.py
@@ -54,11 +54,12 @@
 
 
 def kernel(
-    wave_ref, gate_ref, sens_ref, models_ref, obs_ref, cell_ref, table_ref,
-    out_ref, misfit_ref,
+    wave_in, gate_in, sens_ref, models_in, obs_in, cell_in, table_in,
+    gradient_ref, final_ref,
+    wave_ref, gate_ref, models_ref, obs_ref, cell_ref, table_ref,
     buf, tiles, gathered, wide, expanded, onehot, model_t, cells_t, grads, xrecv, zsend, zrecv, tsend, trecv,
     square_row, square_rows, misfit_row, misfit_rows, final_row, final_rows,
-    bulk_send, bulk_recv, send, recv, pair_send, pair_recv,
+    bulk_send, bulk_recv, send, recv, pair_send, pair_recv, load,
 ):
     tile = lax.axis_index("tile")
     f = lax.axis_index("freq")
@@ -66,8 +67,6 @@
     chunks = buf.shape[0]
     soundings = chunks * ROWS
     gates = obs_ref.shape[1]
-    total = NT * NF * soundings * gates
-    ncells = NT * NF * ROWS
 
     def plane(i):
         return {"freq": lax.rem(x + i // NZ, NX) * NZ + lax.rem(z + i % NZ, NZ)}
@@ -80,11 +79,21 @@
             src_ref=src, dst_ref=dst, send_sem=send_sem, recv_sem=recv_sem, device_id=device, device_id_type=MESH
         ).start()
 
+    loads = [
+        pltpu.make_async_copy(src, dst, load.at[i])
+        for i, (src, dst) in enumerate((
+            (models_in, models_ref), (cell_in, cell_ref), (gate_in, gate_ref),
+            (wave_in, wave_ref), (table_in, table_ref), (obs_in.at[0], obs_ref),
+        ))
+    ]
+    for copy in loads:
+        copy.start()
     barrier = pltpu.get_barrier_semaphore()
     for i in range(1, NF):
         pl.semaphore_signal(barrier, inc=1, device_id=plane(i), device_id_type=MESH)
     for i in range(1, NT):
         pl.semaphore_signal(barrier, inc=1, device_id=other_tile(i), device_id_type=MESH)
+    loads[0].wait()
     pl.semaphore_wait(barrier, NF + NT - 2)
 
     for i in range(1, NT):
@@ -100,6 +109,8 @@
 
     send_chunk(0)
 
+    for copy in loads[1:]:
+        copy.wait()
     cells = cell_ref[...]
     block = lax.shift_right_logical(cells, 8)
     partner = jnp.max(jnp.where(block != tile, block, -1), axis=1, keepdims=True)
@@ -134,7 +145,7 @@
     big_high, big_low = split(jnp.where(same, big, 0.0))
     wide[0] = big_high
     wide[1] = big_low
-    expanded[...] = nn(spread, obs_ref[0], HIGH)
+    expanded[...] = nt(spread, obs_ref[...], HIGH)
 
     await_bytes(gathered.at[0, pl.ds(0, NZ - 1)], recv.at[1])
     for i in range(1, NX):
@@ -177,6 +188,8 @@
         hot = onehot[pl.ds(b * half, half), :]
         part = nt(hot, grad_high) + nt(hot, grad_low)
         grads[b] = part.reshape(NX, NZ, ROWS, -1)
+        if b == 0:
+            await_bytes(xrecv.at[1, pl.ds(0, NX - 1)], pair_send.at[0, 1])
         for i in range(1, NX):
             p = lax.rem(x + i, NX)
             put(grads.at[b, p], xrecv.at[b, x], pair_send.at[0, b], pair_recv.at[0, b], plane(i * NZ))
@@ -217,11 +230,8 @@
         put(final_row, final_rows.at[tile], send.at[6], recv.at[6], other_tile(i))
     final_rows[tile] = final_row[...]
     await_bytes(final_rows.at[pl.ds(0, NT - 1)], recv.at[6])
-    final = jnp.sum(final_rows[...], axis=0)
-    misfit = final[:, members:] / (2.0 * total)
-    scale = jnp.sqrt(final[:, :members] / ncells + EPSILON)
-    out_ref[...] = models_ref[...] - STEP_LENGTH * (misfit / scale) * gradient
-    misfit_ref[...] = misfit
+    gradient_ref[...] = gradient
+    final_ref[...] = jnp.sum(final_rows[...], axis=0)
 
     for c in range(chunks):
         await_bytes(buf.at[c, pl.ds(0, NF - 1)], bulk_send.at[c])
@@ -233,8 +243,16 @@
     await_bytes(square_rows.at[pl.ds(0, NF - 1)], send.at[5])
     await_bytes(final_rows.at[pl.ds(0, NT - 1)], send.at[6])
     for b in range(2):
-        await_bytes(xrecv.at[b, pl.ds(0, NX - 1)], pair_send.at[0, b])
         await_bytes(zrecv.at[b, pl.ds(0, NZ - 1)], pair_send.at[1, b])
+    await_bytes(xrecv.at[0, pl.ds(0, NX - 1)], pair_send.at[0, 0])
+
+
+def finish(total, ncells, models_ref, gradient_ref, final_ref, out_ref, misfit_ref):
+    members = models_ref.shape[1]
+    misfit = final_ref[:, pl.ds(members, members)] / (2.0 * total)
+    scale = jnp.sqrt(final_ref[:, pl.ds(0, members)] / ncells + EPSILON)
+    out_ref[...] = models_ref[...] - STEP_LENGTH * (misfit / scale) * gradient_ref[...]
+    misfit_ref[...] = misfit
 
 
 def body(sensitivity, models, observed, waveform, cell_index, gate_index):
@@ -243,14 +261,20 @@
     ncell = cell_index.shape[1]
     chunks = sensitivity.shape[3] // NF // ROWS
     table = jnp.asarray(kernel_table(NF, waveform.shape[0]))
-    vmem, smem = pl.BlockSpec(memory_space=pltpu.VMEM), pl.BlockSpec(memory_space=pltpu.SMEM)
+    hbm, vmem = pl.BlockSpec(memory_space=pl.ANY), pl.BlockSpec(memory_space=pltpu.VMEM)
     dma = pltpu.SemaphoreType.DMA
-    updated, misfit = pl.pallas_call(
+    gradient, final = pl.pallas_call(
         kernel,
-        out_shape=(jax.ShapeDtypeStruct((owned, members), F32), jax.ShapeDtypeStruct((1, members), F32)),
-        in_specs=[smem, smem, pl.BlockSpec(memory_space=pl.ANY), vmem, vmem, vmem, vmem],
+        out_shape=(jax.ShapeDtypeStruct((owned, members), F32), jax.ShapeDtypeStruct((1, 2 * members), F32)),
+        in_specs=[hbm] * 7,
         out_specs=(vmem, vmem),
         scratch_shapes=[
+            pltpu.SMEM(waveform.shape, F32),
+            pltpu.SMEM(gate_index.shape, jnp.int32),
+            pltpu.VMEM(models.shape, F32),
+            pltpu.VMEM((observed.shape[2], gates), F32),
+            pltpu.VMEM(cell_index.shape, jnp.int32),
+            pltpu.VMEM(table.shape, F32),
             pltpu.VMEM((chunks, NF, 2, ROWS, ncell), F32),
             pltpu.VMEM((NT, ROWS, members), F32),
             pltpu.VMEM((NX, NZ, 2, ROWS, members), F32),
@@ -271,10 +295,17 @@
             pltpu.VMEM((NF, 1, members), F32),
             pltpu.VMEM((1, 2 * members), F32),
             pltpu.VMEM((NT, 1, 2 * members), F32),
-            dma((chunks,)), dma((chunks,)), dma((7,)), dma((7,)), dma((2, 2)), dma((2, 2)),
+            dma((chunks,)), dma((chunks,)), dma((7,)), dma((7,)), dma((2, 2)), dma((2, 2)), dma((6,)),
         ],
         compiler_params=pltpu.CompilerParams(collective_id=0, has_side_effects=True, vmem_limit_bytes=60 << 20),
-    )(waveform, gate_index, sensitivity, models, observed, cell_index, table)
+    )(waveform, gate_index, sensitivity, models, jnp.swapaxes(observed, 1, 2), cell_index, table)
+    devices = NT * NF
+    updated, misfit = pl.pallas_call(
+        functools.partial(finish, NT * sensitivity.shape[3] * gates, owned * devices),
+        out_shape=(jax.ShapeDtypeStruct((owned, members), F32), jax.ShapeDtypeStruct((1, members), F32)),
+        in_specs=[vmem] * 3,
+        out_specs=(vmem, vmem),
+    )(models, gradient, final)
     return updated, misfit[0]
 
 

time: 140 us -> 137 us (0.979)
  local copies, waits for them, and re-layouts: 3.89 us -> 0 us
    unnamed x3 -> x0, local copies, waits for them, and re-layouts: 3.89 us -> none
where the time goes in v2:
time: 137 us
  Pallas kernels  136 us (99%)
    pallas_call x1, Pallas kernels, body(): pl.pallas_call(kernel, out_shape=(jax.ShapeDtypeStruct((owned, members),...  135 us

profile of v2, /device:TPU:1, one launch (start us, length us, event | category | flops | bytes accessed | tf_op | source)
XLA Modules:
  0.0 136.8 jit_solution(841161233661961129)
XLA Ops:
  0.6 134.8 %shard_map.86 = (f32[8,256]{1,0:T(8,128)}, f32[1,512]{1,0:T(1,128)}) custom-call(f32[128]{0:T(128)} %wave_in.1, s32[40]{0:T(128)} %gate_in.1, f32[1,1,2,1024,512]{4,3,2,1,0:T(8,128)} %sens_ref.1, f32[8,256]{1,0:T(8,128)} %models_ref.1, f32[1,32,40]{2,1,0:T(8,128)} %bitcast.2, s32[1,512]{1,0:T(1,128)} %cell_in.1, f32[64,128]{1,0:T(8,128)} %constant.2.clone.table_in), custom_call_target="tpu_custom_call" | custom-call | tf_op jit(solution)/shard_map/pallas_call | solution.py:266
  135.5 1.3 shard_map.87

commit v3 on v2

--- a/solution.py
+++ b/solution.py
@@ -18,6 +18,7 @@
 NF = NX * NZ
 ROWS = 8
 F32, BF16 = jnp.float32, jnp.bfloat16
+NEAR_Z, FAR_Z, ALONG_X = [1, 2, NZ - 2, NZ - 1], [3, 4, 5], [NZ, 2 * NZ, 3 * NZ]
 
 
 def kernel_table(freqs, samples):
@@ -57,9 +58,10 @@
     wave_in, gate_in, sens_ref, models_in, obs_in, cell_in, table_in,
     gradient_ref, final_ref,
     wave_ref, gate_ref, models_ref, obs_ref, cell_ref, table_ref,
-    buf, tiles, gathered, wide, expanded, onehot, model_t, cells_t, grads, xrecv, zsend, zrecv, tsend, trecv,
-    square_row, square_rows, misfit_row, misfit_rows, final_row, final_rows,
-    bulk_send, bulk_recv, send, recv, pair_send, pair_recv, load,
+    buf, tiles, gathered, wide, expanded, onehot, model_t, cells_t, lent, lent_x, lent_sum, lent_z, own, own_z, own_sum, own_x,
+    shared, partner_row, partners,
+    square_row, square_rows, misfit_row, misfit_tiles, misfit_sum, misfit_rows,
+    bulk_send, bulk_recv, send, recv, pair_send, pair_recv, load, known,
 ):
     tile = lax.axis_index("tile")
     f = lax.axis_index("freq")
@@ -89,25 +91,37 @@
     for copy in loads:
         copy.start()
     barrier = pltpu.get_barrier_semaphore()
-    for i in range(1, NF):
+    for i in NEAR_Z + ALONG_X:
         pl.semaphore_signal(barrier, inc=1, device_id=plane(i), device_id_type=MESH)
     for i in range(1, NT):
         pl.semaphore_signal(barrier, inc=1, device_id=other_tile(i), device_id_type=MESH)
     loads[0].wait()
-    pl.semaphore_wait(barrier, NF + NT - 2)
+    pl.semaphore_wait(barrier, len(NEAR_Z + ALONG_X) + NT - 1)
 
     for i in range(1, NT):
         put(models_ref, tiles.at[tile], send.at[0], recv.at[0], other_tile(i))
 
-    def send_chunk(c):
-        for i in range(1, NF):
+    def send_chunk(c, peers=range(1, NF)):
+        for i in peers:
             p = plane(i)
             start = pl.multiple_of(p["freq"] * soundings + c * ROWS, ROWS)
             put(sens_ref.at[0, 0, :, pl.ds(start, ROWS), :], buf.at[c, f], bulk_send.at[c], bulk_recv.at[c], p)
+
+    def keep_chunk(c):
         start = pl.multiple_of(f * soundings + c * ROWS, ROWS)
         pltpu.make_async_copy(sens_ref.at[0, 0, :, pl.ds(start, ROWS), :], buf.at[c, f], bulk_recv.at[c]).start()
 
-    send_chunk(0)
+    send_chunk(0, NEAR_Z + ALONG_X)
+    for i in (2, NZ - 2):
+        pl.semaphore_signal(known.at[0], inc=1, device_id=plane(i), device_id_type=MESH)
+    pl.semaphore_wait(known.at[0], 2)
+    for i in ALONG_X:
+        pl.semaphore_signal(known.at[1], inc=1, device_id=plane(i), device_id_type=MESH)
+    send_chunk(0, FAR_Z)
+    pl.semaphore_wait(known.at[1], len(ALONG_X))
+    send_chunk(0, [i for i in range(1, NF) if i not in NEAR_Z + ALONG_X + FAR_Z])
+    for c in range(chunks):
+        keep_chunk(c)
 
     for copy in loads[1:]:
         copy.wait()
@@ -118,6 +132,10 @@
     ncell = cells.shape[1]
     onehot[...] = jnp.where(iota((ncell, ncell), 0) == local, 1.0, 0.0).astype(BF16)
 
+    partner_row[...] = jnp.broadcast_to(partner.astype(F32), partner_row.shape)
+    for i in range(1, NT):
+        put(partner_row, partners.at[tile], send.at[6], recv.at[6], other_tile(i))
+    partners[tile] = partner_row[...]
     tiles[tile] = models_ref[...]
     await_bytes(tiles.at[pl.ds(0, NT - 1)], recv.at[0])
     borrowed = jnp.zeros_like(models_ref)
@@ -184,54 +202,73 @@
 
     grad_high, grad_low = split(cells_t[...])
     half = NF * ROWS
-    for b in (1, 0):
+
+    def global_rows(b):
         hot = onehot[pl.ds(b * half, half), :]
-        part = nt(hot, grad_high) + nt(hot, grad_low)
-        grads[b] = part.reshape(NX, NZ, ROWS, -1)
-        if b == 0:
-            await_bytes(xrecv.at[1, pl.ds(0, NX - 1)], pair_send.at[0, 1])
-        for i in range(1, NX):
-            p = lax.rem(x + i, NX)
-            put(grads.at[b, p], xrecv.at[b, x], pair_send.at[0, b], pair_recv.at[0, b], plane(i * NZ))
+        return (nt(hot, grad_high) + nt(hot, grad_low)).reshape(NX, NZ, ROWS, -1)
+
+    lent[...] = global_rows(1)
+    for i in range(1, NX):
+        p = lax.rem(x + i, NX)
+        put(lent.at[p], lent_x.at[x], pair_send.at[0], pair_recv.at[0], plane(i * NZ))
+    own[...] = jnp.swapaxes(global_rows(0), 0, 1)
+    for i in range(1, NZ):
+        p = lax.rem(z + i, NZ)
+        put(own.at[p], own_z.at[z], pair_send.at[1], pair_recv.at[1], plane(i))
+    for i in range(1, NT):
+        put(misfit_row, misfit_tiles.at[tile], send.at[7], recv.at[7], other_tile(i))
+
+    lent_x[x] = lent[x]
+    await_bytes(lent_x.at[pl.ds(0, NX - 1)], pair_recv.at[0])
+    lent_sum[...] = (lent_x[0] + lent_x[1]) + (lent_x[2] + lent_x[3])
+    for i in range(1, NZ):
+        p = lax.rem(z + i, NZ)
+        put(lent_sum.at[p], lent_z.at[z], pair_send.at[2], pair_recv.at[2], plane(i))
+    own_z[z] = own[z]
+    await_bytes(own_z.at[pl.ds(0, NZ - 1)], pair_recv.at[1])
+    own_sum[...] = jnp.sum(own_z[...], axis=0)
+    for i in range(1, NX):
+        p = lax.rem(x + i, NX)
+        put(own_sum.at[p], own_x.at[x], pair_send.at[3], pair_recv.at[3], plane(i * NZ))
+    lent_z[z] = lent_sum[z]
+    await_bytes(lent_z.at[pl.ds(0, NZ - 1)], pair_recv.at[2])
+    shared[tile, 1] = jnp.sum(lent_z[...], axis=0)
+    for i in range(1, NT):
+        put(shared.at[tile, 1], shared.at[tile, 1], send.at[4], recv.at[4], other_tile(i))
+    own_x[x] = own_sum[x]
+    await_bytes(own_x.at[pl.ds(0, NX - 1)], pair_recv.at[3])
+    shared[tile, 0] = (own_x[0] + own_x[1]) + (own_x[2] + own_x[3])
+    for i in range(1, NT):
+        put(shared.at[tile, 0], shared.at[tile, 0], send.at[8], recv.at[8], other_tile(i))
+    misfit_tiles[tile] = misfit_row[...]
+    await_bytes(misfit_tiles.at[pl.ds(0, NT - 1)], recv.at[7])
+    misfit_sum[...] = jnp.sum(misfit_tiles[...], axis=0)
     for i in range(1, NF):
-        put(misfit_row, misfit_rows.at[f], send.at[3], recv.at[3], plane(i))
-    for b in (1, 0):
-        xrecv[b, x] = grads[b, x]
-        await_bytes(xrecv.at[b, pl.ds(0, NX - 1)], pair_recv.at[0, b])
-        zsend[b] = (xrecv[b, 0] + xrecv[b, 1]) + (xrecv[b, 2] + xrecv[b, 3])
-        for i in range(1, NZ):
-            p = lax.rem(z + i, NZ)
-            put(zsend.at[b, p], zrecv.at[b, z], pair_send.at[1, b], pair_recv.at[1, b], plane(i))
-    sums = []
-    for b in (1, 0):
-        zrecv[b, z] = zsend[b, z]
-        await_bytes(zrecv.at[b, pl.ds(0, NZ - 1)], pair_recv.at[1, b])
-        sums.append(jnp.sum(zrecv[b], axis=0))
-        if b == 1:
-            for t in range(NT):
-                tsend[t] = jnp.where(partner == t, sums[0], 0.0)
-            for i in range(1, NT):
-                put(tsend.at[lax.rem(tile + i, NT)], trecv.at[tile], send.at[4], recv.at[4], other_tile(i))
-    trecv[tile] = jnp.zeros_like(sums[0])
-    await_bytes(trecv.at[pl.ds(0, NT - 1)], recv.at[4])
-    gradient = sums[1] + jnp.sum(trecv[...], axis=0)
-
-    square_row[...] = jnp.sum(gradient * gradient, axis=0, keepdims=True)
+        put(misfit_sum, misfit_rows.at[f], send.at[3], recv.at[3], plane(i))
+    await_bytes(partners.at[pl.ds(0, NT - 1)], recv.at[6])
+    await_bytes(shared.at[pl.ds(0, NT - 1), 1], recv.at[4])
+    await_bytes(shared.at[pl.ds(0, NT - 1), 0], recv.at[8])
+
+    def gradient_of(t, own_rows):
+        for lender in range(NT):
+            own_rows = own_rows + jnp.where(partners[lender][:, 0:1] == t, shared[lender, 1], 0.0)
+        return own_rows
+
+    squares = jnp.zeros_like(models_ref)
+    for t in range(NT):
+        rows_of = gradient_of(float(t), shared[t, 0])
+        squares = squares + rows_of * rows_of
+    square_row[...] = jnp.sum(squares, axis=0, keepdims=True)
     for i in range(1, NF):
         put(square_row, square_rows.at[f], send.at[5], recv.at[5], plane(i))
+    gradient_ref[...] = gradient_of(tile.astype(F32), shared[tile, 0])
     square_rows[f] = square_row[...]
-    misfit_rows[f] = misfit_row[...]
+    misfit_rows[f] = misfit_sum[...]
     await_bytes(misfit_rows.at[pl.ds(0, NF - 1)], recv.at[3])
     members = misfit_row.shape[1]
-    final_row[:, pl.ds(members, members)] = jnp.sum(misfit_rows[...], axis=0)
+    final_ref[:, pl.ds(members, members)] = jnp.sum(misfit_rows[...], axis=0)
     await_bytes(square_rows.at[pl.ds(0, NF - 1)], recv.at[5])
-    final_row[:, pl.ds(0, members)] = jnp.sum(square_rows[...], axis=0)
-    for i in range(1, NT):
-        put(final_row, final_rows.at[tile], send.at[6], recv.at[6], other_tile(i))
-    final_rows[tile] = final_row[...]
-    await_bytes(final_rows.at[pl.ds(0, NT - 1)], recv.at[6])
-    gradient_ref[...] = gradient
-    final_ref[...] = jnp.sum(final_rows[...], axis=0)
+    final_ref[:, pl.ds(0, members)] = jnp.sum(square_rows[...], axis=0)
 
     for c in range(chunks):
         await_bytes(buf.at[c, pl.ds(0, NF - 1)], bulk_send.at[c])
@@ -239,12 +276,15 @@
     await_bytes(gathered.at[0, pl.ds(0, NZ - 1)], send.at[1])
     await_bytes(gathered.at[pl.ds(0, NX - 1)], send.at[2])
     await_bytes(misfit_rows.at[pl.ds(0, NF - 1)], send.at[3])
-    await_bytes(trecv.at[pl.ds(0, NT - 1)], send.at[4])
+    await_bytes(shared.at[pl.ds(0, NT - 1), 1], send.at[4])
+    await_bytes(shared.at[pl.ds(0, NT - 1), 0], send.at[8])
+    await_bytes(misfit_tiles.at[pl.ds(0, NT - 1)], send.at[7])
     await_bytes(square_rows.at[pl.ds(0, NF - 1)], send.at[5])
-    await_bytes(final_rows.at[pl.ds(0, NT - 1)], send.at[6])
-    for b in range(2):
-        await_bytes(zrecv.at[b, pl.ds(0, NZ - 1)], pair_send.at[1, b])
-    await_bytes(xrecv.at[0, pl.ds(0, NX - 1)], pair_send.at[0, 0])
+    await_bytes(partners.at[pl.ds(0, NT - 1)], send.at[6])
+    await_bytes(lent_x.at[pl.ds(0, NX - 1)], pair_send.at[0])
+    await_bytes(own_z.at[pl.ds(0, NZ - 1)], pair_send.at[1])
+    await_bytes(lent_z.at[pl.ds(0, NZ - 1)], pair_send.at[2])
+    await_bytes(own_x.at[pl.ds(0, NX - 1)], pair_send.at[3])
 
 
 def finish(total, ncells, models_ref, gradient_ref, final_ref, out_ref, misfit_ref):
@@ -283,19 +323,24 @@
             pltpu.VMEM((ncell, ncell), BF16),
             pltpu.VMEM((2, members, ncell), BF16),
             pltpu.VMEM((members, ncell), F32),
-            pltpu.VMEM((2, NX, NZ, ROWS, members), F32),
-            pltpu.VMEM((2, NX, NZ, ROWS, members), F32),
-            pltpu.VMEM((2, NZ, ROWS, members), F32),
-            pltpu.VMEM((2, NZ, ROWS, members), F32),
-            pltpu.VMEM((NT, ROWS, members), F32),
-            pltpu.VMEM((NT, ROWS, members), F32),
+            pltpu.VMEM((NX, NZ, ROWS, members), F32),
+            pltpu.VMEM((NX, NZ, ROWS, members), F32),
+            pltpu.VMEM((NZ, ROWS, members), F32),
+            pltpu.VMEM((NZ, ROWS, members), F32),
+            pltpu.VMEM((NZ, NX, ROWS, members), F32),
+            pltpu.VMEM((NZ, NX, ROWS, members), F32),
+            pltpu.VMEM((NX, ROWS, members), F32),
+            pltpu.VMEM((NX, ROWS, members), F32),
+            pltpu.VMEM((NT, 2, ROWS, members), F32),
+            pltpu.VMEM((1, 128), F32),
+            pltpu.VMEM((NT, 1, 128), F32),
             pltpu.VMEM((1, members), F32),
             pltpu.VMEM((NF, 1, members), F32),
             pltpu.VMEM((1, members), F32),
+            pltpu.VMEM((NT, 1, members), F32),
+            pltpu.VMEM((1, members), F32),
             pltpu.VMEM((NF, 1, members), F32),
-            pltpu.VMEM((1, 2 * members), F32),
-            pltpu.VMEM((NT, 1, 2 * members), F32),
-            dma((chunks,)), dma((chunks,)), dma((7,)), dma((7,)), dma((2, 2)), dma((2, 2)), dma((6,)),
+            dma((chunks,)), dma((chunks,)), dma((9,)), dma((9,)), dma((4,)), dma((4,)), dma((6,)), pltpu.SemaphoreType.REGULAR((2,)),
         ],
         compiler_params=pltpu.CompilerParams(collective_id=0, has_side_effects=True, vmem_limit_bytes=60 << 20),
     )(waveform, gate_index, sensitivity, models, jnp.swapaxes(observed, 1, 2), cell_index, table)

time: 137 us -> 134 us (0.978)
  Pallas kernels: 136 us -> 133 us
    pallas_call x1, Pallas kernels: 135 us -> 132 us  [body(): pl.pallas_call(kernel, out_shape=(jax.ShapeDtypeStruct((owned, members),...]
where the time goes in v3:
time: 134 us
  Pallas kernels  133 us (99%)
    pallas_call x1, Pallas kernels, body(): pl.pallas_call(kernel, out_shape=(jax.ShapeDtypeStruct((owned, members),...  132 us

profile of v3, /device:TPU:1, one launch (start us, length us, event | category | flops | bytes accessed | tf_op | source)
XLA Modules:
  0.0 134.1 jit_solution(6615070167339301638)
XLA Ops:
  0.6 132.1 %shard_map.86 = (f32[8,256]{1,0:T(8,128)}, f32[1,512]{1,0:T(1,128)}) custom-call(f32[128]{0:T(128)} %wave_in.1, s32[40]{0:T(128)} %gate_in.1, f32[1,1,2,1024,512]{4,3,2,1,0:T(8,128)} %sens_ref.1, f32[8,256]{1,0:T(8,128)} %models_ref.1, f32[1,32,40]{2,1,0:T(8,128)} %bitcast.2, s32[1,512]{1,0:T(1,128)} %cell_in.1, f32[64,128]{1,0:T(8,128)} %constant.2.clone.table_in), custom_call_target="tpu_custom_call" | custom-call | tf_op jit(solution)/shard_map/pallas_call | solution.py:306
  132.7 1.3 shard_map.87

commit v4 on v3

--- a/solution.py
+++ b/solution.py
@@ -58,10 +58,10 @@
     wave_in, gate_in, sens_ref, models_in, obs_in, cell_in, table_in,
     gradient_ref, final_ref,
     wave_ref, gate_ref, models_ref, obs_ref, cell_ref, table_ref,
-    buf, tiles, gathered, wide, expanded, onehot, model_t, cells_t, lent, lent_x, lent_sum, lent_z, own, own_z, own_sum, own_x,
+    buf, tiles, gathered, wide, expanded, onehot, model_t, rows_ref, cells_t, lent, lent_x, lent_sum, lent_z, own, own_z, own_sum, own_x,
     shared, partner_row, partners,
     square_row, square_rows, misfit_row, misfit_tiles, misfit_sum, misfit_rows,
-    bulk_send, bulk_recv, send, recv, pair_send, pair_recv, load, known,
+    bulk_send, bulk_recv, send, recv, pair_send, pair_recv, load, known, ring_send, ring_recv,
 ):
     tile = lax.axis_index("tile")
     f = lax.axis_index("freq")
@@ -143,9 +143,19 @@
         borrowed = jnp.where(partner == t, tiles[t], borrowed)
     gathered[x, z, 0] = models_ref[...]
     gathered[x, z, 1] = borrowed
-    for i in range(1, NZ):
-        put(gathered.at[x, z], gathered.at[x, z], send.at[1], recv.at[1], plane(i))
-    send_chunk(1)
+
+    def pass_on(step):
+        down, up = lax.rem(z - step + 1 + NZ, NZ), lax.rem(z + step - 1, NZ)
+        for to, block_z, part in ((1, down, 0), (NZ - 1, up, 1)):
+            block_ref = gathered.at[x, block_z] if 2 * step < NZ else gathered.at[x, block_z, part]
+            put(block_ref, block_ref, ring_send.at[step - 1], ring_recv.at[step - 1], plane(to))
+
+    def passed(step, sems):
+        await_bytes(gathered.at[0, pl.ds(0, 2)] if 2 * step < NZ else gathered.at[0, 0], sems.at[step - 1])
+
+    pass_on(1)
+    first, second = range(1, NF // 2), range(NF // 2, NF)
+    send_chunk(1, first)
 
     samples = table_ref.shape[1]
     rows = iota((gates, samples), 0)
@@ -165,10 +175,18 @@
     wide[1] = big_low
     expanded[...] = nt(spread, obs_ref[...], HIGH)
 
-    await_bytes(gathered.at[0, pl.ds(0, NZ - 1)], recv.at[1])
+    passed(1, ring_recv)
+    pass_on(2)
+    send_chunk(1, second)
+    passed(2, ring_recv)
+    pass_on(3)
+    send_chunk(2, first)
+    passed(3, ring_recv)
+    pass_on(4)
+    send_chunk(2, second)
+    passed(4, ring_recv)
     for i in range(1, NX):
         put(gathered.at[x], gathered.at[x], send.at[2], recv.at[2], plane(i * NZ))
-    send_chunk(2)
     send_chunk(3)
 
     await_bytes(gathered.at[pl.ds(0, NX - 1)], recv.at[2])
@@ -186,15 +204,22 @@
     cells_t[...] = jnp.zeros_like(cells_t)
     misfit_row[...] = jnp.zeros_like(misfit_row)
 
+    rows_ref[...] = jnp.zeros_like(rows_ref)
+
+    def add_squares():
+        rows_t = rows_ref[...]
+        misfit_row[...] += nt(jnp.ones((8, rows_t.shape[1]), F32), rows_t * rows_t, HIGH)[0:1]
+
     def chunk(c, carry):
+        add_squares()
+        seen = expanded[...]
+        seen = jnp.where(iota(seen.shape, 1) == c * ROWS + (iota(seen.shape, 0) & 7), seen, 0.0)
+        seen_row = nt(jnp.ones((8, seen.shape[1]), F32), seen, HIGH)[0:1]
         await_bytes(buf.at[c], bulk_recv.at[c])
         block_s = split(buf[c].reshape(fps * ROWS, ncell))
         operator = split(three(nn, (wide[0], wide[1]), block_s))
-        seen = expanded[...]
-        seen = jnp.where(iota(seen.shape, 1) == c * ROWS + (iota(seen.shape, 0) & 7), seen, 0.0)
-        seen_row = nt(jnp.ones((8, seen.shape[1]), F32), seen, HIGH)[0:1]
         rows_t = three(nt, (model_t[0], model_t[1]), operator) - seen_row
-        misfit_row[...] += nt(jnp.ones((8, rows_t.shape[1]), F32), rows_t * rows_t, HIGH)[0:1]
+        rows_ref[...] = rows_t
         cells_t[...] += three(nn, split(rows_t), operator)
         return carry
 
@@ -215,6 +240,7 @@
     for i in range(1, NZ):
         p = lax.rem(z + i, NZ)
         put(own.at[p], own_z.at[z], pair_send.at[1], pair_recv.at[1], plane(i))
+    add_squares()
     for i in range(1, NT):
         put(misfit_row, misfit_tiles.at[tile], send.at[7], recv.at[7], other_tile(i))
 
@@ -273,7 +299,8 @@
     for c in range(chunks):
         await_bytes(buf.at[c, pl.ds(0, NF - 1)], bulk_send.at[c])
     await_bytes(tiles.at[pl.ds(0, NT - 1)], send.at[0])
-    await_bytes(gathered.at[0, pl.ds(0, NZ - 1)], send.at[1])
+    for step in range(1, NZ // 2 + 1):
+        passed(step, ring_send)
     await_bytes(gathered.at[pl.ds(0, NX - 1)], send.at[2])
     await_bytes(misfit_rows.at[pl.ds(0, NF - 1)], send.at[3])
     await_bytes(shared.at[pl.ds(0, NT - 1), 1], send.at[4])
@@ -322,6 +349,7 @@
             pltpu.VMEM((gates * ROWS, chunks * ROWS), F32),
             pltpu.VMEM((ncell, ncell), BF16),
             pltpu.VMEM((2, members, ncell), BF16),
+            pltpu.VMEM((members, gates * ROWS), F32),
             pltpu.VMEM((members, ncell), F32),
             pltpu.VMEM((NX, NZ, ROWS, members), F32),
             pltpu.VMEM((NX, NZ, ROWS, members), F32),
@@ -340,7 +368,7 @@
             pltpu.VMEM((NT, 1, members), F32),
             pltpu.VMEM((1, members), F32),
             pltpu.VMEM((NF, 1, members), F32),
-            dma((chunks,)), dma((chunks,)), dma((9,)), dma((9,)), dma((4,)), dma((4,)), dma((6,)), pltpu.SemaphoreType.REGULAR((2,)),
+            dma((chunks,)), dma((chunks,)), dma((9,)), dma((9,)), dma((4,)), dma((4,)), dma((6,)), pltpu.SemaphoreType.REGULAR((2,)), dma((NZ // 2,)), dma((NZ // 2,)),
         ],
         compiler_params=pltpu.CompilerParams(collective_id=0, has_side_effects=True, vmem_limit_bytes=60 << 20),
     )(waveform, gate_index, sensitivity, models, jnp.swapaxes(observed, 1, 2), cell_index, table)

time: 134 us -> 133 us (level)
  no operation moved by 1% of the time
where the time goes in v4:
time: 133 us
  Pallas kernels  132 us (99%)
    pallas_call x1, Pallas kernels, body(): pl.pallas_call(kernel, out_shape=(jax.ShapeDtypeStruct((owned, members),...  131 us

profile of v4, /device:TPU:1, one launch (start us, length us, event | category | flops | bytes accessed | tf_op | source)
XLA Modules:
  0.0 132.8 jit_solution(4633673921869056422)
XLA Ops:
  0.6 130.8 %shard_map.86 = (f32[8,256]{1,0:T(8,128)}, f32[1,512]{1,0:T(1,128)}) custom-call(f32[128]{0:T(128)} %wave_in.1, s32[40]{0:T(128)} %gate_in.1, f32[1,1,2,1024,512]{4,3,2,1,0:T(8,128)} %sens_ref.1, f32[8,256]{1,0:T(8,128)} %models_ref.1, f32[1,32,40]{2,1,0:T(8,128)} %bitcast.2, s32[1,512]{1,0:T(1,128)} %cell_in.1, f32[64,128]{1,0:T(8,128)} %constant.2.clone.table_in), custom_call_target="tpu_custom_call" | custom-call | tf_op jit(solution)/shard_map/pallas_call | solution.py:333
  131.4 1.3 %shard_map.87 = (f32[8,256]{1,0:T(8,128)}, f32[1,256]{1,0:T(1,128)}) custom-call(f32[8,256]{1,0:T(8,128)} %models_ref.1, f32[8,256]{1,0:T(8,128)} %get-tuple-element.6.gradient_ref, f32[1,512]{1,0:T(1,128)} %get-tuple-element.7.final_ref), custom_call_target="tpu_custom_call" | custom-call | tf_op jit(solution)/shard_map/pallas_call | solution.py:376

commit v5 on v4

--- a/solution.py
+++ b/solution.py
@@ -18,6 +18,7 @@
 NF = NX * NZ
 ROWS = 8
 F32, BF16 = jnp.float32, jnp.bfloat16
+STAGES = ((0, 2, 0, 2), (2, 1, 4, 5))
 NEAR_Z, FAR_Z, ALONG_X = [1, 2, NZ - 2, NZ - 1], [3, 4, 5], [NZ, 2 * NZ, 3 * NZ]
 
 
@@ -58,7 +59,8 @@
     wave_in, gate_in, sens_ref, models_in, obs_in, cell_in, table_in,
     gradient_ref, final_ref,
     wave_ref, gate_ref, models_ref, obs_ref, cell_ref, table_ref,
-    buf, tiles, gathered, wide, expanded, onehot, model_t, rows_ref, cells_t, lent, lent_x, lent_sum, lent_z, own, own_z, own_sum, own_x,
+    buf, tiles, gathered, wide, expanded, onehot, model_t, rows_ref, cells_t, major, major_x, major_sum, major_z,
+    minor, minor_z, minor_sum, minor_x,
     shared, partner_row, partners,
     square_row, square_rows, misfit_row, misfit_tiles, misfit_sum, misfit_rows,
     bulk_send, bulk_recv, send, recv, pair_send, pair_recv, load, known, ring_send, ring_recv,
@@ -226,54 +228,65 @@
     lax.fori_loop(0, chunks, chunk, 0)
 
     grad_high, grad_low = split(cells_t[...])
-    half = NF * ROWS
+    half, lanes = NF * ROWS, cells_t.shape[0] // 2
 
     def global_rows(b):
         hot = onehot[pl.ds(b * half, half), :]
         return (nt(hot, grad_high) + nt(hot, grad_low)).reshape(NX, NZ, ROWS, -1)
 
-    lent[...] = global_rows(1)
+    lent = global_rows(1)
+    major[:, 0] = lent[..., :lanes]
+    major[:, 1] = lent[..., lanes:]
     for i in range(1, NX):
         p = lax.rem(x + i, NX)
-        put(lent.at[p], lent_x.at[x], pair_send.at[0], pair_recv.at[0], plane(i * NZ))
-    own[...] = jnp.swapaxes(global_rows(0), 0, 1)
+        put(major.at[p, pl.ds(0, 2)], major_x.at[x, pl.ds(0, 2)], pair_send.at[0], pair_recv.at[0], plane(i * NZ))
+    own = global_rows(0)
+    minor[...] = jnp.swapaxes(own[..., lanes:], 0, 1)
     for i in range(1, NZ):
         p = lax.rem(z + i, NZ)
-        put(own.at[p], own_z.at[z], pair_send.at[1], pair_recv.at[1], plane(i))
+        put(minor.at[p], minor_z.at[z], pair_send.at[1], pair_recv.at[1], plane(i))
+    major[:, 2] = own[..., :lanes]
+    for i in range(1, NX):
+        p = lax.rem(x + i, NX)
+        put(major.at[p, 2], major_x.at[x, 2], pair_send.at[4], pair_recv.at[4], plane(i * NZ))
     add_squares()
     for i in range(1, NT):
         put(misfit_row, misfit_tiles.at[tile], send.at[7], recv.at[7], other_tile(i))
 
-    lent_x[x] = lent[x]
-    await_bytes(lent_x.at[pl.ds(0, NX - 1)], pair_recv.at[0])
-    lent_sum[...] = (lent_x[0] + lent_x[1]) + (lent_x[2] + lent_x[3])
-    for i in range(1, NZ):
-        p = lax.rem(z + i, NZ)
-        put(lent_sum.at[p], lent_z.at[z], pair_send.at[2], pair_recv.at[2], plane(i))
-    own_z[z] = own[z]
-    await_bytes(own_z.at[pl.ds(0, NZ - 1)], pair_recv.at[1])
-    own_sum[...] = jnp.sum(own_z[...], axis=0)
+    major_x[x] = major[x]
+    minor_z[z] = minor[z]
+    for first, count, sem_x, sem_z in STAGES:
+        quarters = pl.ds(first, count)
+        await_bytes(major_x.at[pl.ds(0, NX - 1), quarters], pair_recv.at[sem_x])
+        total_x = (major_x[0, quarters] + major_x[1, quarters]) + (major_x[2, quarters] + major_x[3, quarters])
+        major_sum[:, quarters] = jnp.swapaxes(total_x, 0, 1)
+        for i in range(1, NZ):
+            p = lax.rem(z + i, NZ)
+            put(major_sum.at[p, quarters], major_z.at[z, quarters], pair_send.at[sem_z], pair_recv.at[sem_z], plane(i))
+    await_bytes(minor_z.at[pl.ds(0, NZ - 1)], pair_recv.at[1])
+    minor_sum[...] = jnp.sum(minor_z[...], axis=0)
     for i in range(1, NX):
         p = lax.rem(x + i, NX)
-        put(own_sum.at[p], own_x.at[x], pair_send.at[3], pair_recv.at[3], plane(i * NZ))
-    lent_z[z] = lent_sum[z]
-    await_bytes(lent_z.at[pl.ds(0, NZ - 1)], pair_recv.at[2])
-    shared[tile, 1] = jnp.sum(lent_z[...], axis=0)
+        put(minor_sum.at[p], minor_x.at[x], pair_send.at[3], pair_recv.at[3], plane(i * NZ))
+    minor_x[x] = minor_sum[x]
+    await_bytes(minor_x.at[pl.ds(0, NX - 1)], pair_recv.at[3])
+    shared[tile, 0, :, pl.ds(lanes, lanes)] = (minor_x[0] + minor_x[1]) + (minor_x[2] + minor_x[3])
+    major_z[z] = major_sum[z]
+    for first, count, _, sem_z in STAGES:
+        await_bytes(major_z.at[pl.ds(0, NZ - 1), pl.ds(first, count)], pair_recv.at[sem_z])
+    total_z = jnp.sum(major_z[...], axis=0)
+    shared[tile, 1, :, pl.ds(0, lanes)] = total_z[0]
+    shared[tile, 1, :, pl.ds(lanes, lanes)] = total_z[1]
+    shared[tile, 0, :, pl.ds(0, lanes)] = total_z[2]
     for i in range(1, NT):
-        put(shared.at[tile, 1], shared.at[tile, 1], send.at[4], recv.at[4], other_tile(i))
-    own_x[x] = own_sum[x]
-    await_bytes(own_x.at[pl.ds(0, NX - 1)], pair_recv.at[3])
-    shared[tile, 0] = (own_x[0] + own_x[1]) + (own_x[2] + own_x[3])
-    for i in range(1, NT):
-        put(shared.at[tile, 0], shared.at[tile, 0], send.at[8], recv.at[8], other_tile(i))
+        put(shared.at[tile], shared.at[tile], send.at[4], recv.at[4], other_tile(i))
     misfit_tiles[tile] = misfit_row[...]
     await_bytes(misfit_tiles.at[pl.ds(0, NT - 1)], recv.at[7])
     misfit_sum[...] = jnp.sum(misfit_tiles[...], axis=0)
     for i in range(1, NF):
         put(misfit_sum, misfit_rows.at[f], send.at[3], recv.at[3], plane(i))
     await_bytes(partners.at[pl.ds(0, NT - 1)], recv.at[6])
-    await_bytes(shared.at[pl.ds(0, NT - 1), 1], recv.at[4])
-    await_bytes(shared.at[pl.ds(0, NT - 1), 0], recv.at[8])
+    await_bytes(shared.at[pl.ds(0, NT - 1)], recv.at[4])
 
     def gradient_of(t, own_rows):
         for lender in range(NT):
@@ -303,15 +316,15 @@
         passed(step, ring_send)
     await_bytes(gathered.at[pl.ds(0, NX - 1)], send.at[2])
     await_bytes(misfit_rows.at[pl.ds(0, NF - 1)], send.at[3])
-    await_bytes(shared.at[pl.ds(0, NT - 1), 1], send.at[4])
-    await_bytes(shared.at[pl.ds(0, NT - 1), 0], send.at[8])
+    await_bytes(shared.at[pl.ds(0, NT - 1)], send.at[4])
     await_bytes(misfit_tiles.at[pl.ds(0, NT - 1)], send.at[7])
     await_bytes(square_rows.at[pl.ds(0, NF - 1)], send.at[5])
     await_bytes(partners.at[pl.ds(0, NT - 1)], send.at[6])
-    await_bytes(lent_x.at[pl.ds(0, NX - 1)], pair_send.at[0])
-    await_bytes(own_z.at[pl.ds(0, NZ - 1)], pair_send.at[1])
-    await_bytes(lent_z.at[pl.ds(0, NZ - 1)], pair_send.at[2])
-    await_bytes(own_x.at[pl.ds(0, NX - 1)], pair_send.at[3])
+    for first, count, sem_x, sem_z in STAGES:
+        await_bytes(major_x.at[pl.ds(0, NX - 1), pl.ds(first, count)], pair_send.at[sem_x])
+        await_bytes(major_z.at[pl.ds(0, NZ - 1), pl.ds(first, count)], pair_send.at[sem_z])
+    await_bytes(minor_z.at[pl.ds(0, NZ - 1)], pair_send.at[1])
+    await_bytes(minor_x.at[pl.ds(0, NX - 1)], pair_send.at[3])
 
 
 def finish(total, ncells, models_ref, gradient_ref, final_ref, out_ref, misfit_ref):
@@ -351,14 +364,14 @@
             pltpu.VMEM((2, members, ncell), BF16),
             pltpu.VMEM((members, gates * ROWS), F32),
             pltpu.VMEM((members, ncell), F32),
-            pltpu.VMEM((NX, NZ, ROWS, members), F32),
-            pltpu.VMEM((NX, NZ, ROWS, members), F32),
-            pltpu.VMEM((NZ, ROWS, members), F32),
-            pltpu.VMEM((NZ, ROWS, members), F32),
-            pltpu.VMEM((NZ, NX, ROWS, members), F32),
-            pltpu.VMEM((NZ, NX, ROWS, members), F32),
-            pltpu.VMEM((NX, ROWS, members), F32),
-            pltpu.VMEM((NX, ROWS, members), F32),
+            pltpu.VMEM((NX, 3, NZ, ROWS, members // 2), F32),
+            pltpu.VMEM((NX, 3, NZ, ROWS, members // 2), F32),
+            pltpu.VMEM((NZ, 3, ROWS, members // 2), F32),
+            pltpu.VMEM((NZ, 3, ROWS, members // 2), F32),
+            pltpu.VMEM((NZ, NX, ROWS, members // 2), F32),
+            pltpu.VMEM((NZ, NX, ROWS, members // 2), F32),
+            pltpu.VMEM((NX, ROWS, members // 2), F32),
+            pltpu.VMEM((NX, ROWS, members // 2), F32),
             pltpu.VMEM((NT, 2, ROWS, members), F32),
             pltpu.VMEM((1, 128), F32),
             pltpu.VMEM((NT, 1, 128), F32),
@@ -368,7 +381,7 @@
             pltpu.VMEM((NT, 1, members), F32),
             pltpu.VMEM((1, members), F32),
             pltpu.VMEM((NF, 1, members), F32),
-            dma((chunks,)), dma((chunks,)), dma((9,)), dma((9,)), dma((4,)), dma((4,)), dma((6,)), pltpu.SemaphoreType.REGULAR((2,)), dma((NZ // 2,)), dma((NZ // 2,)),
+            dma((chunks,)), dma((chunks,)), dma((8,)), dma((8,)), dma((6,)), dma((6,)), dma((6,)), pltpu.SemaphoreType.REGULAR((2,)), dma((NZ // 2,)), dma((NZ // 2,)),
         ],
         compiler_params=pltpu.CompilerParams(collective_id=0, has_side_effects=True, vmem_limit_bytes=60 << 20),
     )(waveform, gate_index, sensitivity, models, jnp.swapaxes(observed, 1, 2), cell_index, table)

time: 133 us -> 131 us (0.985)
  Pallas kernels: 132 us -> 130 us
    pallas_call x1, Pallas kernels: 131 us -> 128 us  [body(): pl.pallas_call(kernel, out_shape=(jax.ShapeDtypeStruct((owned, members),...]
where the time goes in v5:
time: 131 us; the launch traced here: 130 us
  Pallas kernels  130 us (99%)
    pallas_call x1, Pallas kernels, body(): pl.pallas_call(kernel, out_shape=(jax.ShapeDtypeStruct((owned, members),...  128 us

profile of v5, /device:TPU:1, one launch (start us, length us, event | category | flops | bytes accessed | tf_op | source)
XLA Modules:
  0.0 130.4 jit_solution(2098326562503109639)
XLA Ops:
  0.6 128.4 %shard_map.86 = (f32[8,256]{1,0:T(8,128)}, f32[1,512]{1,0:T(1,128)}) custom-call(f32[128]{0:T(128)} %wave_in.1, s32[40]{0:T(128)} %gate_in.1, f32[1,1,2,1024,512]{4,3,2,1,0:T(8,128)} %sens_ref.1, f32[8,256]{1,0:T(8,128)} %models_ref.1, f32[1,32,40]{2,1,0:T(8,128)} %bitcast.2, s32[1,512]{1,0:T(1,128)} %cell_in.1, f32[64,128]{1,0:T(8,128)} %constant.2.clone.table_in), custom_call_target="tpu_custom_call" | custom-call | tf_op jit(solution)/shard_map/pallas_call | solution.py:346
  129.0 1.3 %shard_map.87 = (f32[8,256]{1,0:T(8,128)}, f32[1,256]{1,0:T(1,128)}) custom-call(f32[8,256]{1,0:T(8,128)} %models_ref.1, f32[8,256]{1,0:T(8,128)} %get-tuple-element.6.gradient_ref, f32[1,512]{1,0:T(1,128)} %get-tuple-element.7.final_ref), custom_call_target="tpu_custom_call" | custom-call | tf_op jit(solution)/shard_map/pallas_call | solution.py:389

commit v6 on v5

--- a/solution.py
+++ b/solution.py
@@ -18,6 +18,8 @@
 NF = NX * NZ
 ROWS = 8
 F32, BF16 = jnp.float32, jnp.bfloat16
+EARLY = range(NZ, 3 * NZ)
+FAR_FIRST = sorted(range(1, NF), key=lambda i: (-min(i % NZ, NZ - i % NZ), -min(i // NZ, NX - i // NZ), i))
 STAGES = ((0, 2, 0, 2), (2, 1, 4, 5))
 NEAR_Z, FAR_Z, ALONG_X = [1, 2, NZ - 2, NZ - 1], [3, 4, 5], [NZ, 2 * NZ, 3 * NZ]
 
@@ -107,11 +109,11 @@
         for i in peers:
             p = plane(i)
             start = pl.multiple_of(p["freq"] * soundings + c * ROWS, ROWS)
-            put(sens_ref.at[0, 0, :, pl.ds(start, ROWS), :], buf.at[c, f], bulk_send.at[c], bulk_recv.at[c], p)
+            put(sens_ref.at[0, 0, :, pl.ds(start, ROWS), :], buf.at[c, f], bulk_send.at[c], bulk_recv.at[c, int(i not in EARLY)], p)
 
     def keep_chunk(c):
         start = pl.multiple_of(f * soundings + c * ROWS, ROWS)
-        pltpu.make_async_copy(sens_ref.at[0, 0, :, pl.ds(start, ROWS), :], buf.at[c, f], bulk_recv.at[c]).start()
+        pltpu.make_async_copy(sens_ref.at[0, 0, :, pl.ds(start, ROWS), :], buf.at[c, f], bulk_recv.at[c, 1]).start()
 
     send_chunk(0, NEAR_Z + ALONG_X)
     for i in (2, NZ - 2):
@@ -189,7 +191,7 @@
     passed(4, ring_recv)
     for i in range(1, NX):
         put(gathered.at[x], gathered.at[x], send.at[2], recv.at[2], plane(i * NZ))
-    send_chunk(3)
+    send_chunk(3, sorted(FAR_FIRST, key=lambda i: i not in EARLY))
 
     await_bytes(gathered.at[pl.ds(0, NX - 1)], recv.at[2])
     for b in range(2):
@@ -217,9 +219,20 @@
         seen = expanded[...]
         seen = jnp.where(iota(seen.shape, 1) == c * ROWS + (iota(seen.shape, 0) & 7), seen, 0.0)
         seen_row = nt(jnp.ones((8, seen.shape[1]), F32), seen, HIGH)[0:1]
-        await_bytes(buf.at[c], bulk_recv.at[c])
-        block_s = split(buf[c].reshape(fps * ROWS, ncell))
-        operator = split(three(nn, (wide[0], wide[1]), block_s))
+        operator = None
+        for late, offsets in enumerate(((1, 2), (3, 0))):
+            await_bytes(buf.at[c, pl.ds(0, NF // 2)], bulk_recv.at[c, late])
+            blocks, columns = [], [[], []]
+            for offset in offsets:
+                source = lax.rem(x - offset + NX, NX)
+                width = NZ * 2 * ROWS
+                blocks.append(buf[c, pl.ds(source * NZ, NZ)].reshape(width, ncell))
+                for k in range(2):
+                    columns[k].append(wide[k, :, pl.ds(pl.multiple_of(source * width, width), width)])
+            block_s = split(jnp.concatenate(blocks, axis=0))
+            part = three(nn, [jnp.concatenate(cols, axis=1) for cols in columns], block_s)
+            operator = part if operator is None else operator + part
+        operator = split(operator)
         rows_t = three(nt, (model_t[0], model_t[1]), operator) - seen_row
         rows_ref[...] = rows_t
         cells_t[...] += three(nn, split(rows_t), operator)
@@ -237,16 +250,16 @@
     lent = global_rows(1)
     major[:, 0] = lent[..., :lanes]
     major[:, 1] = lent[..., lanes:]
-    for i in range(1, NX):
+    for i in (2, 1, 3):
         p = lax.rem(x + i, NX)
         put(major.at[p, pl.ds(0, 2)], major_x.at[x, pl.ds(0, 2)], pair_send.at[0], pair_recv.at[0], plane(i * NZ))
     own = global_rows(0)
     minor[...] = jnp.swapaxes(own[..., lanes:], 0, 1)
-    for i in range(1, NZ):
+    for i in (4, 3, 5, 2, 6, 1, 7):
         p = lax.rem(z + i, NZ)
         put(minor.at[p], minor_z.at[z], pair_send.at[1], pair_recv.at[1], plane(i))
     major[:, 2] = own[..., :lanes]
-    for i in range(1, NX):
+    for i in (2, 1, 3):
         p = lax.rem(x + i, NX)
         put(major.at[p, 2], major_x.at[x, 2], pair_send.at[4], pair_recv.at[4], plane(i * NZ))
     add_squares()
@@ -260,33 +273,36 @@
         await_bytes(major_x.at[pl.ds(0, NX - 1), quarters], pair_recv.at[sem_x])
         total_x = (major_x[0, quarters] + major_x[1, quarters]) + (major_x[2, quarters] + major_x[3, quarters])
         major_sum[:, quarters] = jnp.swapaxes(total_x, 0, 1)
-        for i in range(1, NZ):
+        for i in (4, 3, 5, 2, 6, 1, 7):
             p = lax.rem(z + i, NZ)
             put(major_sum.at[p, quarters], major_z.at[z, quarters], pair_send.at[sem_z], pair_recv.at[sem_z], plane(i))
     await_bytes(minor_z.at[pl.ds(0, NZ - 1)], pair_recv.at[1])
     minor_sum[...] = jnp.sum(minor_z[...], axis=0)
-    for i in range(1, NX):
+    for i in (2, 1, 3):
         p = lax.rem(x + i, NX)
         put(minor_sum.at[p], minor_x.at[x], pair_send.at[3], pair_recv.at[3], plane(i * NZ))
     minor_x[x] = minor_sum[x]
+    major_z[z] = major_sum[z]
+    await_bytes(major_z.at[pl.ds(0, NZ - 1), pl.ds(0, 2)], pair_recv.at[STAGES[0][3]])
+    lent_z = jnp.sum(major_z[:, pl.ds(0, 2)], axis=0)
+    shared[tile, 1, :, pl.ds(0, lanes)] = lent_z[0]
+    shared[tile, 1, :, pl.ds(lanes, lanes)] = lent_z[1]
+    for i in range(1, NT):
+        put(shared.at[tile, 1], shared.at[tile, 1], send.at[8], recv.at[8], other_tile(i))
     await_bytes(minor_x.at[pl.ds(0, NX - 1)], pair_recv.at[3])
     shared[tile, 0, :, pl.ds(lanes, lanes)] = (minor_x[0] + minor_x[1]) + (minor_x[2] + minor_x[3])
-    major_z[z] = major_sum[z]
-    for first, count, _, sem_z in STAGES:
-        await_bytes(major_z.at[pl.ds(0, NZ - 1), pl.ds(first, count)], pair_recv.at[sem_z])
-    total_z = jnp.sum(major_z[...], axis=0)
-    shared[tile, 1, :, pl.ds(0, lanes)] = total_z[0]
-    shared[tile, 1, :, pl.ds(lanes, lanes)] = total_z[1]
-    shared[tile, 0, :, pl.ds(0, lanes)] = total_z[2]
-    for i in range(1, NT):
-        put(shared.at[tile], shared.at[tile], send.at[4], recv.at[4], other_tile(i))
+    await_bytes(major_z.at[pl.ds(0, NZ - 1), pl.ds(2, 1)], pair_recv.at[STAGES[1][3]])
+    shared[tile, 0, :, pl.ds(0, lanes)] = jnp.sum(major_z[:, 2], axis=0)
+    for i in range(1, NT):
+        put(shared.at[tile, 0], shared.at[tile, 0], send.at[4], recv.at[4], other_tile(i))
     misfit_tiles[tile] = misfit_row[...]
     await_bytes(misfit_tiles.at[pl.ds(0, NT - 1)], recv.at[7])
     misfit_sum[...] = jnp.sum(misfit_tiles[...], axis=0)
     for i in range(1, NF):
         put(misfit_sum, misfit_rows.at[f], send.at[3], recv.at[3], plane(i))
     await_bytes(partners.at[pl.ds(0, NT - 1)], recv.at[6])
-    await_bytes(shared.at[pl.ds(0, NT - 1)], recv.at[4])
+    await_bytes(shared.at[pl.ds(0, NT - 1), 1], recv.at[8])
+    await_bytes(shared.at[pl.ds(0, NT - 1), 0], recv.at[4])
 
     def gradient_of(t, own_rows):
         for lender in range(NT):
@@ -298,7 +314,7 @@
         rows_of = gradient_of(float(t), shared[t, 0])
         squares = squares + rows_of * rows_of
     square_row[...] = jnp.sum(squares, axis=0, keepdims=True)
-    for i in range(1, NF):
+    for i in FAR_FIRST:
         put(square_row, square_rows.at[f], send.at[5], recv.at[5], plane(i))
     gradient_ref[...] = gradient_of(tile.astype(F32), shared[tile, 0])
     square_rows[f] = square_row[...]
@@ -316,7 +332,8 @@
         passed(step, ring_send)
     await_bytes(gathered.at[pl.ds(0, NX - 1)], send.at[2])
     await_bytes(misfit_rows.at[pl.ds(0, NF - 1)], send.at[3])
-    await_bytes(shared.at[pl.ds(0, NT - 1)], send.at[4])
+    await_bytes(shared.at[pl.ds(0, NT - 1), 1], send.at[8])
+    await_bytes(shared.at[pl.ds(0, NT - 1), 0], send.at[4])
     await_bytes(misfit_tiles.at[pl.ds(0, NT - 1)], send.at[7])
     await_bytes(square_rows.at[pl.ds(0, NF - 1)], send.at[5])
     await_bytes(partners.at[pl.ds(0, NT - 1)], send.at[6])
@@ -381,7 +398,7 @@
             pltpu.VMEM((NT, 1, members), F32),
             pltpu.VMEM((1, members), F32),
             pltpu.VMEM((NF, 1, members), F32),
-            dma((chunks,)), dma((chunks,)), dma((8,)), dma((8,)), dma((6,)), dma((6,)), dma((6,)), pltpu.SemaphoreType.REGULAR((2,)), dma((NZ // 2,)), dma((NZ // 2,)),
+            dma((chunks,)), dma((chunks, 2)), dma((9,)), dma((9,)), dma((6,)), dma((6,)), dma((6,)), pltpu.SemaphoreType.REGULAR((2,)), dma((NZ // 2,)), dma((NZ // 2,)),
         ],
         compiler_params=pltpu.CompilerParams(collective_id=0, has_side_effects=True, vmem_limit_bytes=60 << 20),
     )(waveform, gate_index, sensitivity, models, jnp.swapaxes(observed, 1, 2), cell_index, table)

time: 131 us -> 129 us (0.985)
  Pallas kernels: 130 us -> 128 us
    pallas_call x1, Pallas kernels: 128 us -> 127 us  [body(): pl.pallas_call(kernel, out_shape=(jax.ShapeDtypeStruct((owned, members),...]
where the time goes in v6:
time: 129 us
  Pallas kernels  128 us (99%)
    pallas_call x1, Pallas kernels, body(): pl.pallas_call(kernel, out_shape=(jax.ShapeDtypeStruct((owned, members),...  127 us

profile of v6, /device:TPU:1, one launch (start us, length us, event | category | flops | bytes accessed | tf_op | source)
XLA Modules:
  0.0 128.8 jit_solution(15026873709896727183)
XLA Ops:
  0.6 126.8 %shard_map.86 = (f32[8,256]{1,0:T(8,128)}, f32[1,512]{1,0:T(1,128)}) custom-call(f32[128]{0:T(128)} %wave_in.1, s32[40]{0:T(128)} %gate_in.1, f32[1,1,2,1024,512]{4,3,2,1,0:T(8,128)} %sens_ref.1, f32[8,256]{1,0:T(8,128)} %models_ref.1, f32[1,32,40]{2,1,0:T(8,128)} %bitcast.2, s32[1,512]{1,0:T(1,128)} %cell_in.1, f32[64,128]{1,0:T(8,128)} %constant.2.clone.table_in), custom_call_target="tpu_custom_call" | custom-call | tf_op jit(solution)/shard_map/pallas_call | solution.py:363
  127.5 1.3 %shard_map.87 = (f32[8,256]{1,0:T(8,128)}, f32[1,256]{1,0:T(1,128)}) custom-call(f32[8,256]{1,0:T(8,128)} %models_ref.1, f32[8,256]{1,0:T(8,128)} %get-tuple-element.6.gradient_ref, f32[1,512]{1,0:T(1,128)} %get-tuple-element.7.final_ref), custom_call_target="tpu_custom_call" | custom-call | tf_op jit(solution)/shard_map/pallas_call | solution.py:406

commit v7 on v6

--- a/solution.py
+++ b/solution.py
@@ -20,7 +20,7 @@
 F32, BF16 = jnp.float32, jnp.bfloat16
 EARLY = range(NZ, 3 * NZ)
 FAR_FIRST = sorted(range(1, NF), key=lambda i: (-min(i % NZ, NZ - i % NZ), -min(i // NZ, NX - i // NZ), i))
-STAGES = ((0, 2, 0, 2), (2, 1, 4, 5))
+STAGES = ((0, 1, 0, 2), (1, 1, 6, 7), (2, 1, 4, 5))
 NEAR_Z, FAR_Z, ALONG_X = [1, 2, NZ - 2, NZ - 1], [3, 4, 5], [NZ, 2 * NZ, 3 * NZ]
 
 
@@ -158,7 +158,7 @@
         await_bytes(gathered.at[0, pl.ds(0, 2)] if 2 * step < NZ else gathered.at[0, 0], sems.at[step - 1])
 
     pass_on(1)
-    first, second = range(1, NF // 2), range(NF // 2, NF)
+    first, second = EARLY, [i for i in FAR_FIRST if i not in EARLY]
     send_chunk(1, first)
 
     samples = table_ref.shape[1]
@@ -248,11 +248,12 @@
         return (nt(hot, grad_high) + nt(hot, grad_low)).reshape(NX, NZ, ROWS, -1)
 
     lent = global_rows(1)
-    major[:, 0] = lent[..., :lanes]
-    major[:, 1] = lent[..., lanes:]
-    for i in (2, 1, 3):
-        p = lax.rem(x + i, NX)
-        put(major.at[p, pl.ds(0, 2)], major_x.at[x, pl.ds(0, 2)], pair_send.at[0], pair_recv.at[0], plane(i * NZ))
+    for q in range(2):
+        major[:, q] = lent[..., q * lanes:(q + 1) * lanes]
+        for i in (2, 1, 3):
+            p = lax.rem(x + i, NX)
+            sem = STAGES[q][2]
+            put(major.at[p, q], major_x.at[x, q], pair_send.at[sem], pair_recv.at[sem], plane(i * NZ))
     own = global_rows(0)
     minor[...] = jnp.swapaxes(own[..., lanes:], 0, 1)
     for i in (4, 3, 5, 2, 6, 1, 7):
@@ -283,7 +284,8 @@
         put(minor_sum.at[p], minor_x.at[x], pair_send.at[3], pair_recv.at[3], plane(i * NZ))
     minor_x[x] = minor_sum[x]
     major_z[z] = major_sum[z]
-    await_bytes(major_z.at[pl.ds(0, NZ - 1), pl.ds(0, 2)], pair_recv.at[STAGES[0][3]])
+    for q in range(2):
+        await_bytes(major_z.at[pl.ds(0, NZ - 1), pl.ds(q, 1)], pair_recv.at[STAGES[q][3]])
     lent_z = jnp.sum(major_z[:, pl.ds(0, 2)], axis=0)
     shared[tile, 1, :, pl.ds(0, lanes)] = lent_z[0]
     shared[tile, 1, :, pl.ds(lanes, lanes)] = lent_z[1]
@@ -291,7 +293,7 @@
         put(shared.at[tile, 1], shared.at[tile, 1], send.at[8], recv.at[8], other_tile(i))
     await_bytes(minor_x.at[pl.ds(0, NX - 1)], pair_recv.at[3])
     shared[tile, 0, :, pl.ds(lanes, lanes)] = (minor_x[0] + minor_x[1]) + (minor_x[2] + minor_x[3])
-    await_bytes(major_z.at[pl.ds(0, NZ - 1), pl.ds(2, 1)], pair_recv.at[STAGES[1][3]])
+    await_bytes(major_z.at[pl.ds(0, NZ - 1), pl.ds(2, 1)], pair_recv.at[STAGES[2][3]])
     shared[tile, 0, :, pl.ds(0, lanes)] = jnp.sum(major_z[:, 2], axis=0)
     for i in range(1, NT):
         put(shared.at[tile, 0], shared.at[tile, 0], send.at[4], recv.at[4], other_tile(i))
@@ -398,7 +400,7 @@
             pltpu.VMEM((NT, 1, members), F32),
             pltpu.VMEM((1, members), F32),
             pltpu.VMEM((NF, 1, members), F32),
-            dma((chunks,)), dma((chunks, 2)), dma((9,)), dma((9,)), dma((6,)), dma((6,)), dma((6,)), pltpu.SemaphoreType.REGULAR((2,)), dma((NZ // 2,)), dma((NZ // 2,)),
+            dma((chunks,)), dma((chunks, 2)), dma((9,)), dma((9,)), dma((8,)), dma((8,)), dma((6,)), pltpu.SemaphoreType.REGULAR((2,)), dma((NZ // 2,)), dma((NZ // 2,)),
         ],
         compiler_params=pltpu.CompilerParams(collective_id=0, has_side_effects=True, vmem_limit_bytes=60 << 20),
     )(waveform, gate_index, sensitivity, models, jnp.swapaxes(observed, 1, 2), cell_index, table)

time: 129 us -> 129 us (level)
  no operation moved by 1% of the time
where the time goes in v7:
time: 129 us
  Pallas kernels  128 us (99%)
    pallas_call x1, Pallas kernels, body(): pl.pallas_call(kernel, out_shape=(jax.ShapeDtypeStruct((owned, members),...  127 us

profile of v7, /device:TPU:1, one launch (start us, length us, event | category | flops | bytes accessed | tf_op | source)
XLA Modules:
  0.0 128.8 jit_solution(18292911219604342260)
XLA Ops:
  0.6 126.8 %shard_map.86 = (f32[8,256]{1,0:T(8,128)}, f32[1,512]{1,0:T(1,128)}) custom-call(f32[128]{0:T(128)} %wave_in.1, s32[40]{0:T(128)} %gate_in.1, f32[1,1,2,1024,512]{4,3,2,1,0:T(8,128)} %sens_ref.1, f32[8,256]{1,0:T(8,128)} %models_ref.1, f32[1,32,40]{2,1,0:T(8,128)} %bitcast.2, s32[1,512]{1,0:T(1,128)} %cell_in.1, f32[64,128]{1,0:T(8,128)} %constant.2.clone.table_in), custom_call_target="tpu_custom_call" | custom-call | tf_op jit(solution)/shard_map/pallas_call | solution.py:365
  127.5 1.3 %shard_map.87 = (f32[8,256]{1,0:T(8,128)}, f32[1,256]{1,0:T(1,128)}) custom-call(f32[8,256]{1,0:T(8,128)} %models_ref.1, f32[8,256]{1,0:T(8,128)} %get-tuple-element.6.gradient_ref, f32[1,512]{1,0:T(1,128)} %get-tuple-element.7.final_ref), custom_call_target="tpu_custom_call" | custom-call | tf_op jit(solution)/shard_map/pallas_call | solution.py:408
